TPU v7x, 256 devices: a whole 4x4x8 slice. The times are simulated.
256 devices in a mesh: dp: 8 (over x, y_hi), mp: 32 (over z, y_lo, core).
Axes of the slice: x: 4, y: 4 (y_hi: 2, y_lo: 2; y = y_hi * 2 + y_lo), z: 8, core: 2. Of those that a mesh axis runs over, the one named last changes fastest.
Arguments:
- hidden: bfloat16 [64, 128, 18432], P('dp', None, 'mp'), may hold values from -400 to 400
- cotangent: bfloat16 [64, 128, 4608], P('dp', 'mp'), may hold values from -8 to 8
- w_down: bfloat16 [18432, 4608], P('mp', 'dp'), may hold values from -0.046875 to 0.046875
- lengths: int32 [64], P('dp'), may hold values from 1 to 128, 6144 in all
Outputs:
- weight_grad: float32 [18432, 4608], P('mp', 'dp')
- d_hidden: bfloat16 [64, 128, 18432], P('dp', None, 'mp')
All inputs are finite; a program needn't handle non-finite values. No bound on the sum of `lengths` on one device may be relied on, other than what follows from the above.
Results may differ from a plain program's by a relative error of at most 0.003.
Values may be sent and summed in bfloat16 or wider, within the bound.
No kernel may reach another device: no remote copies, remote signals or barrier semaphores. Data moves between devices by JAX's collectives and lax.ppermute only.
A program may use at most 256 MiB of HBM per device.

v0:
```python
import math
import jax
import jax.numpy as jnp
from jax import lax
from jax.sharding import PartitionSpec as P


def body(hidden, cotangent, w_down, lengths):
    seqs = hidden.shape[0]
    whole = lax.all_gather(cotangent, "mp", axis=1, tiled=True)
    seq_len = whole.shape[1]
    width = whole.shape[2]
    positions = jnp.arange(seq_len, dtype=jnp.int32)
    keep = positions[None, :] < lengths[:, None]
    masked = jnp.where(keep[:, :, None], whole, jnp.zeros((), whole.dtype))
    flat = masked.reshape(seqs * seq_len, width)
    units = hidden.shape[2]
    part = flat
    grads_in = lax.dot_general(
        part,
        lax.all_gather(w_down, "dp", axis=1, tiled=True),
        (((1,), (1,)), ((), ())),
        preferred_element_type=jnp.float32,
    )
    d_hidden = grads_in.astype(jnp.bfloat16).reshape(seqs, seq_len, units)
    cot_gram = jnp.einsum("bsd,btd->bst", masked, masked, preferred_element_type=jnp.float32)
    hid_gram = jnp.einsum("bsf,btf->bst", hidden, hidden, preferred_element_type=jnp.float32)
    summed = lax.psum(hid_gram.astype(jnp.bfloat16), "mp").astype(jnp.float32)
    sq_norm = jnp.sum(summed * cot_gram, axis=(1, 2))
    full_units = units * lax.axis_size("mp")
    groups = lax.axis_size("dp")
    radius = math.sqrt(full_units * width / (seqs * groups))
    clip_scale = radius / jnp.sqrt(sq_norm + 1e-06)
    share = width // groups
    running = jnp.zeros((share * lax.axis_size("dp"), units), jnp.float32)
    for which in range(seqs):
        part = masked[which]
        running = running + clip_scale[which] * lax.dot_general(
            part, hidden[which], (((0,), (0,)), ((), ())), preferred_element_type=jnp.float32
        )
    local = lax.psum_scatter(running, "dp", scatter_dimension=0, tiled=True)
    weight_grad = local.T
    return (weight_grad, d_hidden)


def solution(mesh):
    in_specs = (P("dp", None, "mp"), P("dp", "mp", None), P("mp", "dp"), P("dp"))
    out_specs = (P("mp", "dp"), P("dp", None, "mp"))
    return jax.shard_map(body, mesh=mesh, in_specs=in_specs, out_specs=out_specs, check_vma=False)
```

profile of v0, /device:TPU:1, one launch (start us, length us, event | category | flops | bytes accessed | tf_op | source)
XLA Modules:
  0.0 570.3 jit_solution(3020541415049871727)
XLA Ops:
  7.2 0.0 all-gather.3.cloned.1.call-start
  7.2 1.7 copy.14
  8.9 0.0 all-gather.3.cloned.1.call-update
  9.0 0.0 all-reduce.2.cloned.1.call-start
  9.0 3.0 convolution_convert_fusion.1
  12.0 0.0 all-reduce.2.cloned.1.call-update
  12.0 0.0 all-gather.5.cloned.1.call-start
  12.1 2.3 copy.16
  14.3 0.0 all-gather.5.cloned.1.call-update
  14.4 0.0 reduce-scatter.2.cloned.1.call-start
  14.4 0.7 iota_compare_fusion
  15.1 71.8 %all-gather.3.cloned.1.call-done = bf16[8,128,4608]{2,0,1:T(8,128)(2,1)} async-done(((bf16[8,4,4608]{2,0,1:T(8,128)(2,1)}), bf16[8,128,4608]{2,0,1:T(8,128)(2,1)}) %all-gather.3.cloned.1.call-update) | async-done | bytes 9437200 | tf_op jit(solution)/shard_map/all_gather | solution.py:10
  86.9 13.3 %copy_select_fusion = bf16[8,128,4608]{2,1,0:T(8,128)(2,1)} fusion(bf16[8,128,4608]{2,0,1:T(8,128)(2,1)} %all-gather.3.cloned.1.call-done, pred[8,128]{1,0:T(8,128)(4,1)S(1)} %iota_compare_fusion), kind=kLoop, calls=%fused_computation.1 | loop fusion | flops 4718592 | bytes 18875392 | tf_op jit(solution)/shard_map/jit(_where)/select_n | solution.py:15
  100.2 0.0 copy-start
  100.2 215.5 %all-reduce.2.cloned.1.call-done = bf16[8,128,128]{2,1,0:T(8,128)(2,1)} async-done(((bf16[8,128,128]{2,1,0:T(8,128)(2,1)}), bf16[8,128,128]{2,1,0:T(8,128)(2,1)}) %all-reduce.2.cloned.1.call-update) | async-done | bytes 262160 | tf_op jit(solution)/shard_map/psum | solution.py:28
  315.7 9.1 %fusion.8 = f32[8]{0:T(128)S(1)} fusion(bf16[8,128,4608]{2,1,0:T(8,128)(2,1)} %copy_select_fusion, bf16[8,128,128]{2,1,0:T(8,128)(2,1)} %all-reduce.2.cloned.1.call-done), kind=kOutput, calls=%fused_computation.22 | convolution fusion | flops 1208352768 | bytes 9699360 | tf_op jit(solution)/shard_map/bsd,btd->bst/dot_general | solution.py:26
  324.7 0.0 slice-start
  324.7 0.7 fusion.25
  325.4 0.0 copy-done
  325.4 0.0 slice-start.1
  325.4 0.0 slice-start.2
  325.4 7.9 %fusion.1 = f32[4608,576]{1,0:T(8,128)} fusion(bf16[8,128,4608]{2,1,0:T(8,128)(2,1)} %copy_select_fusion, bf16[8,128,576]{1,2,0:T(8,128)(2,1)S(1)} %copy-done), kind=kOutput, calls=%fused_computation.9 | convolution fusion | flops 679477248 | bytes 11943936 | tf_op jit(solution)/shard_map/dot_general | solution.py:38
  333.3 0.0 slice-done
  333.3 0.0 slice-done.1
  333.3 0.0 slice-done.2
  333.4 6.1 %fusion.2 = f32[4608,576]{1,0:T(8,128)} fusion(bf16[8,128,4608]{2,1,0:T(8,128)(2,1)S(1)} %bitcast.71, bf16[8,128,576]{1,2,0:T(8,128)(2,1)S(1)} %copy-done), kind=kOutput, calls=%fused_computation.11 | convolution fusion | flops 679477248 | bytes 11943936 | tf_op jit(solution)/shard_map/dot_general | solution.py:38
  339.5 6.2 %fusion.3 = f32[4608,576]{1,0:T(8,128)} fusion(bf16[8,128,4608]{2,1,0:T(8,128)(2,1)S(1)} %bitcast.71, bf16[8,128,576]{1,2,0:T(8,128)(2,1)S(1)} %copy-done), kind=kOutput, calls=%fused_computation.13 | convolution fusion | flops 679477248 | bytes 11943936 | tf_op jit(solution)/shard_map/dot_general | solution.py:38
  345.7 6.0 %fusion.4 = f32[4608,576]{1,0:T(8,128)} fusion(bf16[8,128,4608]{2,1,0:T(8,128)(2,1)S(1)} %bitcast.71, bf16[8,128,576]{1,2,0:T(8,128)(2,1)S(1)} %copy-done), kind=kOutput, calls=%fused_computation.15 | convolution fusion | flops 679477248 | bytes 11943936 | tf_op jit(solution)/shard_map/dot_general | solution.py:38
  351.7 6.1 %fusion.5 = f32[4608,576]{1,0:T(8,128)} fusion(bf16[8,128,4608]{2,1,0:T(8,128)(2,1)S(1)} %bitcast.71, bf16[8,128,576]{1,2,0:T(8,128)(2,1)S(1)} %copy-done), kind=kOutput, calls=%fused_computation.17 | convolution fusion | flops 679477248 | bytes 11943936 | tf_op jit(solution)/shard_map/dot_general | solution.py:38
  357.7 6.4 %fusion.6 = f32[4608,576]{1,0:T(8,128)} fusion(bf16[8,128,4608]{2,1,0:T(8,128)(2,1)S(1)} %bitcast.71, bf16[8,128,576]{1,2,0:T(8,128)(2,1)S(1)} %copy-done), kind=kOutput, calls=%fused_computation.19 | convolution fusion | flops 679477248 | bytes 11943936 | tf_op jit(solution)/shard_map/dot_general | solution.py:38
  364.1 6.0 %fusion.7 = f32[4608,576]{1,0:T(8,128)} fusion(bf16[8,128,4608]{2,1,0:T(8,128)(2,1)S(1)} %bitcast.71, bf16[8,128,576]{1,2,0:T(8,128)(2,1)S(1)} %copy-done), kind=kOutput, calls=%fused_computation.21 | convolution fusion | flops 679477248 | bytes 11943936 | tf_op jit(solution)/shard_map/dot_general | solution.py:38
  370.1 37.4 %multiply_add_fusion = f32[4608,576]{1,0:T(8,128)} fusion(f32[4608,576]{1,0:T(8,128)} %fusion.1, f32[4608,576]{1,0:T(8,128)} %fusion.2, f32[4608,576]{1,0:T(8,128)} %fusion.3, f32[4608,576]{1,0:T(8,128)} %fusion.4, f32[4608,576]{1,0:T(8,128)} %fusion.5, f32[4608,576]{1,0:T(8,128)} %fusion.6, f32[4608,576]{1,0:T(8,128)} %fusion.7, f32[]{:T(128)} %bitcast.21, ...), kind=kOutput, calls=%fused_computation | convolution fusion | flops 719290368 | bytes 94523392 | tf_op jit(solution)/shard_map/dot_general | solution.py:38
  407.5 0.0 reduce-scatter.2.cloned.1.call-update
  407.6 1.7 all-gather.5.cloned.1.call-done
  409.3 10.1 %fusion = bf16[72,8,8,128]{3,2,1,0:T(8,128)(2,1)S(1)} fusion(bf16[1024,4608]{1,0:T(8,128)(2,1)} %bitcast.69, bf16[576,4608]{0,1:T(8,128)(2,1)} %all-gather.5.cloned.1.call-done), kind=kOutput, calls=%fused_computation.3 | convolution fusion | flops 5436407808 | bytes 15925248 | tf_op jit(solution)/shard_map/dot_general | solution.py:19
  419.4 1.2 copy.22
  420.6 140.2 %reduce-scatter.2.cloned.1.call-done = f32[576,576]{1,0:T(8,128)} async-done(((f32[4608,576]{1,0:T(8,128)}), f32[576,576]{1,0:T(8,128)}) %reduce-scatter.2.cloned.1.call-update) | async-done | bytes 1327120 | tf_op jit(solution)/shard_map/reduce_scatter | solution.py:41
  560.8 3.0 copy.17
  (2 shorter events, 0.0 us)
Async XLA Ops:
  7.2 79.8 %all-gather.3.cloned.1.call-start = ((), (), s32[]{:S(2)}) async-start(), calls=%async_computation.2 | async-start | bytes 9732096 | tf_op jit(solution)/shard_map/all_gather | solution.py:10
  9.0 306.7 %all-reduce.2.cloned.1.call-start = ((), (), s32[]{:S(2)}) async-start(), calls=%async_computation.1 | async-start | bytes 524288 | tf_op jit(solution)/shard_map/psum | solution.py:28
  12.0 397.3 %all-gather.5.cloned.1.call-start = ((), (), s32[]{:S(2)}) async-start(), calls=%async_computation.4 | async-start | bytes 6635520 | tf_op jit(solution)/shard_map/all_gather | solution.py:21
  14.4 546.5 %reduce-scatter.2.cloned.1.call-start = ((), (), s32[]{:S(2)}) async-start(), calls=%async_computation.3 | async-start | bytes 13271040 | tf_op jit(solution)/shard_map/reduce_scatter | solution.py:41
  100.2 225.2 %copy-start = (bf16[8,128,576]{1,2,0:T(8,128)(2,1)S(1)}, bf16[8,128,576]{1,2,0:T(8,128)(2,1)}, u32[]{:S(2)}) copy-start(bf16[8,128,576]{1,2,0:T(8,128)(2,1)} %param.4) | copy-start | bytes 3538948
  324.7 8.6 %slice-start = ((s8[9437184]{0:T(1024)(128)(4,1)}), s8[4194304]{0:T(1024)(128)(4,1)S(1)}, s32[]{:S(2)}) async-start(s8[9437184]{0:T(1024)(128)(4,1)} %bitcast.70), calls=%async_computation.5 | async-start | bytes 8388608
  325.4 7.9 %slice-start.1 = ((s8[9437184]{0:T(1024)(128)(4,1)}), s8[4194304]{0:T(1024)(128)(4,1)S(1)}, s32[]{:S(2)}) async-start(s8[9437184]{0:T(1024)(128)(4,1)} %bitcast.70), calls=%async_computation.6 | async-start | bytes 8388608
  325.4 7.9 %slice-start.2 = ((s8[9437184]{0:T(1024)(128)(4,1)}), s8[1048576]{0:T(1024)(128)(4,1)S(1)}, s32[]{:S(2)}) async-start(s8[9437184]{0:T(1024)(128)(4,1)} %bitcast.70), calls=%async_computation.7 | async-start | bytes 2097152
Sparse Core Ops, SparseCore 0:
  10.4 76.4 all-gather.2
  89.5 226.0 all-reduce.1
  318.8 90.3 all-gather.4
  413.3 147.4 reduce-scatter.1
where the time goes:
time: 571 us; the launch traced here: 570 us
  waiting for transfers between devices  429 us (75%)
  matrix products  104 us (18%)
  other arithmetic  14 us (2%)
  between operations  13.8 us (2%)
  local copies, waits for them, and re-layouts  8.89 us (2%)
    psum x1, waiting for transfers between devices, body(): summed = lax.psum(hid_gram.astype(jnp.bfloat16), 'mp').astype(jnp.float32)  215 us
    reduce_scatter x1, waiting for transfers between devices, body(): local = lax.psum_scatter(running, 'dp', scatter_dimension=0, tiled=True)  140 us
    dot_general x8, matrix products, body(): lax.dot_general(part, hidden[which], (((0,), (0,)), ((), ())), preferred_...  82.1 us
    all_gather x1, waiting for transfers between devices, body(): whole = lax.all_gather(cotangent, 'mp', axis=1, tiled=True)  71.8 us
    select_n x1, other arithmetic, body(): masked = jnp.where(keep[:, :, None], whole, jnp.zeros((), whole.dtype))  13.3 us
  transfers between devices with their start and end apart: 4, of which 4 were waited for; matrix products, arithmetic and copies ran while one was open for 21% of the time, Pallas kernels for 0%

commit v1 on v0

--- a/solution.py
+++ b/solution.py
@@ -7,7 +7,9 @@
 
 def body(hidden, cotangent, w_down, lengths):
     seqs = hidden.shape[0]
-    whole = lax.all_gather(cotangent, "mp", axis=1, tiled=True)
+    whole = jnp.concatenate(
+        lax.all_to_all(jnp.stack([cotangent] * lax.axis_size("mp")), "mp", 0, 0), axis=1
+    )
     seq_len = whole.shape[1]
     width = whole.shape[2]
     positions = jnp.arange(seq_len, dtype=jnp.int32)

time: 571 us -> 605 us (1.060)
  local copies, waits for them, and re-layouts: 8.89 us -> 82.8 us
  waiting for transfers between devices: 429 us -> 382 us
  starting transfers between devices: 0.16 us -> 11.4 us
    all_to_all x0 -> x1, waiting for transfers between devices: none -> 206 us  [body(): lax.all_to_all(jnp.stack([cotangent] * lax.axis_size('mp')), 'mp', 0, 0)]
    psum x1, waiting for transfers between devices: 215 us -> 62.1 us  [body(): summed = lax.psum(hid_gram.astype(jnp.bfloat16), 'mp').astype(jnp.float32)]
    all_gather x1 -> x0, waiting for transfers between devices: 71.8 us -> none  [body(): whole = lax.all_gather(cotangent, 'mp', axis=1, tiled=True)]
    slice x0 -> x1, local copies, waits for them, and re-layouts: none -> 34.8 us  [body(): part = masked[which]]
    reduce_scatter x1, waiting for transfers between devices: 140 us -> 114 us  [body(): local = lax.psum_scatter(running, 'dp', scatter_dimension=0, tiled=True)]
    reshape x0 -> x2, local copies, waits for them, and re-layouts: none -> 23.4 us  [body(): jnp.concatenate(lax.all_to_all(jnp.stack([cotangent] * lax.axis_size('mp'...]
    all_to_all x0 -> x1, starting transfers between devices: none -> 11.3 us  [body(): lax.all_to_all(jnp.stack([cotangent] * lax.axis_size('mp')), 'mp', 0, 0)]
    all_to_all x0 -> x1, local copies, waits for them, and re-layouts: none -> 9.55 us  [body(): lax.all_to_all(jnp.stack([cotangent] * lax.axis_size('mp')), 'mp', 0, 0)]
  transfers between devices with their start and end apart: 4 -> 4, of which waited for: 4 -> 3; matrix products, arithmetic and copies ran while one was open for 21% -> 30% of each run, Pallas kernels for 0% -> 0%
where the time goes in v1:
time: 605 us; the launch traced here: 604 us
  waiting for transfers between devices  382 us (63%)
  matrix products  105 us (17%)
  local copies, waits for them, and re-layouts  82.8 us (14%)
  between operations  15.6 us (3%)
  starting transfers between devices  11.4 us (2%)
  other arithmetic  8.12 us (1%)
    all_to_all x1, waiting for transfers between devices, body(): lax.all_to_all(jnp.stack([cotangent] * lax.axis_size('mp')), 'mp', 0, 0)  206 us
    reduce_scatter x1, waiting for transfers between devices, body(): local = lax.psum_scatter(running, 'dp', scatter_dimension=0, tiled=True)  114 us
    dot_general x8, matrix products, body(): lax.dot_general(part, hidden[which], (((0,), (0,)), ((), ())), preferred_...  80.8 us
    psum x1, waiting for transfers between devices, body(): summed = lax.psum(hid_gram.astype(jnp.bfloat16), 'mp').astype(jnp.float32)  62.1 us
    slice x1, local copies, waits for them, and re-layouts, body(): part = masked[which]  34.8 us
    reshape x2, local copies, waits for them, and re-layouts, body(): jnp.concatenate(lax.all_to_all(jnp.stack([cotangent] * lax.axis_size('mp'...  23.4 us
  transfers between devices with their start and end apart: 4, of which 3 were waited for; matrix products, arithmetic and copies ran while one was open for 30% of the time, Pallas kernels for 0%

profile of v1, /device:TPU:1, one launch (start us, length us, event | category | flops | bytes accessed | tf_op | source)
XLA Modules:
  0.0 604.4 jit_solution(2320449250424091720)
XLA Ops:
  8.0 8.8 %stack.2 = bf16[32,8,4,4608]{3,2,1,0:T(4,128)(2,1)} broadcast(bf16[8,4,4608]{2,1,0:T(4,128)(2,1)} %param.5), dimensions={1,2,3} | broadcast | bytes 9732096 | tf_op jit(solution)/shard_map/stack | solution.py:11
  16.8 0.0 copy-start
  16.8 11.3 %all-to-all-start = ((bf16[32,8,4,4608]{3,2,1,0:T(4,128)(2,1)}), bf16[32,8,4,4608]{3,2,1,0:T(4,128)(2,1)}, u32[]{:S(2)}, u32[]{:S(2)}) async-start(bf16[32,8,4,4608]{3,2,1,0:T(4,128)(2,1)} %stack.2), calls=%async_computation | async-start | bytes 18874368 | tf_op jit(solution)/shard_map/all_to_all | solution.py:11
  28.2 0.0 copy-start.7
  28.2 0.0 copy-start.8
  28.2 0.0 all-reduce.2.cloned.1.call-start
  28.2 0.0 copy-done
  28.2 1.3 convolution_convert_fusion
  29.5 0.0 all-reduce.2.cloned.1.call-update
  29.6 0.0 all-gather.2.cloned.1.call-start
  29.6 0.0 copy-done.7
  29.6 1.2 copy.23
  30.8 0.0 all-gather.2.cloned.1.call-update
  30.8 0.0 reduce-scatter.2.cloned.1.call-start
  30.9 0.0 copy-done.8
  30.9 0.1 fusion.58
  30.9 0.1 copy.18
  31.1 206.1 %all-to-all-done = bf16[32,8,4,4608]{3,2,1,0:T(4,128)(2,1)} async-done(((bf16[32,8,4,4608]{3,2,1,0:T(4,128)(2,1)}), bf16[32,8,4,4608]{3,2,1,0:T(4,128)(2,1)}, u32[]{:S(2)}, u32[]{:S(2)}) %all-to-all-start) | async-done | bytes 9437216 | tf_op jit(solution)/shard_map/all_to_all | solution.py:11
  237.1 9.5 %copy.77 = bf16[32,8,4,4608]{3,1,2,0:T(8,128)(2,1)} copy(bf16[32,8,4,4608]{3,2,1,0:T(4,128)(2,1)} %all-to-all-done) | data formatting | bytes 18874368 | tf_op jit(solution)/shard_map/all_to_all | solution.py:11
  246.7 8.0 %bitcast_select_fusion = bf16[8,128,4608]{2,0,1:T(8,128)(2,1)} fusion(bf16[32,8,4,4608]{3,1,2,0:T(8,128)(2,1)} %copy.77, pred[8,128]{0,1:T(8,128)(4,1)S(1)} %copy.18), kind=kLoop, calls=%fused_computation.1 | loop fusion | flops 4718592 | bytes 18875392 | tf_op jit(solution)/shard_map/jit(_where)/select_n | solution.py:17
  254.7 34.8 %fusion.59 = (bf16[1,128,4608]{2,0,1:T(2,128)(2,1)}, bf16[1,128,4608]{2,0,1:T(2,128)(2,1)}, bf16[1,128,4608]{2,0,1:T(2,128)(2,1)}, bf16[1,128,4608]{2,0,1:T(2,12...) fusion(bf16[8,128,4608]{2,0,1:T(8,128)(2,1)} %bitcast_select_fusion), kind=kLoop, calls=%fused_computation.58 | loop fusion | bytes 18874368 | tf_op jit(solution)/shard_map/slice | solution.py:39
  289.5 62.1 %all-reduce.2.cloned.1.call-done = bf16[8,128,128]{2,1,0:T(8,128)(2,1)} async-done(((bf16[8,128,128]{2,1,0:T(8,128)(2,1)}), bf16[8,128,128]{2,1,0:T(8,128)(2,1)}) %all-reduce.2.cloned.1.call-update) | async-done | bytes 262160 | tf_op jit(solution)/shard_map/psum | solution.py:30
  351.6 11.8 %fusion.38 = f32[8]{0:T(128)S(1)} fusion(bf16[8,128,4608]{2,0,1:T(8,128)(2,1)} %bitcast_select_fusion, bf16[8,128,128]{2,1,0:T(8,128)(2,1)} %all-reduce.2.cloned.1.call-done), kind=kOutput, calls=%fused_computation.36 | convolution fusion | flops 1208352768 | bytes 9699360 | tf_op jit(solution)/shard_map/bsd,btd->bst/dot_general | solution.py:28
  363.4 0.7 fusion.60
  364.0 0.0 copy-start.5
  364.1 7.9 %fusion.17 = f32[4608,576]{1,0:T(8,128)} fusion(bf16[1,128,4608]{2,0,1:T(2,128)(2,1)} %get-tuple-element.13, bf16[8,128,576]{1,2,0:T(8,128)(2,1)S(1)} %copy-done), kind=kOutput, calls=%fused_computation.15 | convolution fusion | flops 679477248 | bytes 11943936 | tf_op jit(solution)/shard_map/dot_general | solution.py:40
  372.0 0.0 copy-done.5
  372.0 0.0 copy-start.4
  372.0 6.1 %fusion.20 = f32[4608,576]{1,0:T(8,128)} fusion(bf16[1,128,4608]{2,0,1:T(2,128)(2,1)S(1)} %copy-done.5, bf16[8,128,576]{1,2,0:T(8,128)(2,1)S(1)} %copy-done), kind=kOutput, calls=%fused_computation.18 | convolution fusion | flops 679477248 | bytes 13123584 | tf_op jit(solution)/shard_map/dot_general | solution.py:40
  378.1 0.0 copy-done.4
  378.1 0.0 copy-start.3
  378.1 6.0 %fusion.23 = f32[4608,576]{1,0:T(8,128)} fusion(bf16[1,128,4608]{2,0,1:T(2,128)(2,1)S(1)} %copy-done.4, bf16[8,128,576]{1,2,0:T(8,128)(2,1)S(1)} %copy-done), kind=kOutput, calls=%fused_computation.21 | convolution fusion | flops 679477248 | bytes 13123584 | tf_op jit(solution)/shard_map/dot_general | solution.py:40
  384.1 0.0 copy-done.3
  384.1 0.0 copy-start.2
  384.1 6.2 %fusion.26 = f32[4608,576]{1,0:T(8,128)} fusion(bf16[1,128,4608]{2,0,1:T(2,128)(2,1)S(1)} %copy-done.3, bf16[8,128,576]{1,2,0:T(8,128)(2,1)S(1)} %copy-done), kind=kOutput, calls=%fused_computation.24 | convolution fusion | flops 679477248 | bytes 13123584 | tf_op jit(solution)/shard_map/dot_general | solution.py:40
  390.4 0.0 copy-done.2
  390.4 0.0 copy-start.1
  390.4 6.1 %fusion.29 = f32[4608,576]{1,0:T(8,128)} fusion(bf16[1,128,4608]{2,0,1:T(2,128)(2,1)S(1)} %copy-done.2, bf16[8,128,576]{1,2,0:T(8,128)(2,1)S(1)} %copy-done), kind=kOutput, calls=%fused_computation.27 | convolution fusion | flops 679477248 | bytes 13123584 | tf_op jit(solution)/shard_map/dot_general | solution.py:40
  396.5 0.0 copy-done.1
  396.5 6.0 fusion.32
  402.5 0.0 copy-start.6
  402.5 6.0 fusion.35
  408.5 0.0 copy-done.6
  408.5 36.5 %multiply_add_fusion = f32[4608,576]{1,0:T(8,128)} fusion(f32[4608,576]{1,0:T(8,128)} %fusion.17, f32[4608,576]{1,0:T(8,128)} %fusion.20, f32[4608,576]{1,0:T(8,128)} %fusion.23, f32[4608,576]{1,0:T(8,128)} %fusion.26, f32[4608,576]{1,0:T(8,128)} %fusion.29, f32[4608,576]{1,0:T(8,128)} %fusion.32, f32[4608,576]{1,0:T(8,128)} %fusion.35, f32[]{:T(128)} %bitcast.16, ...), kind=kOutput, calls=%fused_computation | convolution fusion | flops 719290368 | bytes 87441440 | tf_op jit(solution)/shard_map/dot_general | solution.py:40
  444.9 0.0 reduce-scatter.2.cloned.1.call-update
  444.9 10.3 %copy.22 = bf16[8,32,4,4608]{3,2,1,0:T(4,128)(2,1)} copy(bf16[8,32,4,4608]{3,0,2,1:T(8,128)(2,1)} %bitcast.73) | data formatting | bytes 18874368 | tf_op jit(solution)/shard_map/reshape | solution.py:10
  455.3 13.1 %reshape.47 = bf16[1024,4608]{1,0:T(8,128)(2,1)} reshape(bf16[8,32,4,4608]{3,2,1,0:T(4,128)(2,1)} %copy.22) | data formatting | bytes 18874368 | tf_op jit(solution)/shard_map/reshape | solution.py:10
  468.4 0.0 all-gather.2.cloned.1.call-done
  468.4 10.7 %fusion.9 = bf16[72,8,8,128]{3,2,1,0:T(8,128)(2,1)S(1)} fusion(bf16[576,4608]{0,1:T(8,128)(2,1)} %all-gather.2.cloned.1.call-done, bf16[1024,4608]{1,0:T(8,128)(2,1)} %reshape.47, pred[1024]{0:T(1024)(128)(4,1)S(1)} %get-tuple-element.20), kind=kOutput, calls=%fused_computation.9 | convolution fusion | flops 5441126400 | bytes 15926272 | tf_op jit(solution)/shard_map/dot_general | solution.py:21
  479.1 1.2 copy.76
  480.3 113.7 %reduce-scatter.2.cloned.1.call-done = f32[576,576]{1,0:T(8,128)} async-done(((f32[4608,576]{1,0:T(8,128)}), f32[576,576]{1,0:T(8,128)}) %reduce-scatter.2.cloned.1.call-update) | async-done | bytes 1327120 | tf_op jit(solution)/shard_map/reduce_scatter | solution.py:43
  594.0 3.0 copy.24
  (1 shorter events, 0.0 us)
Async XLA Ops:
  16.8 11.4 %copy-start = (bf16[8,128,576]{1,2,0:T(8,128)(2,1)S(1)}, bf16[8,128,576]{1,2,0:T(8,128)(2,1)}, u32[]{:S(2)}) copy-start(bf16[8,128,576]{1,2,0:T(8,128)(2,1)} %param.4) | copy-start | bytes 3538948
  16.8 220.3 %all-to-all-start = ((bf16[32,8,4,4608]{3,2,1,0:T(4,128)(2,1)}), bf16[32,8,4,4608]{3,2,1,0:T(4,128)(2,1)}, u32[]{:S(2)}, u32[]{:S(2)}) async-start(bf16[32,8,4,4608]{3,2,1,0:T(4,128)(2,1)} %stack.2), calls=%async_computation | async-start | bytes 18874368 | tf_op jit(solution)/shard_map/all_to_all | solution.py:11
  28.2 1.4 copy-start.7
  28.2 2.7 copy-start.8
  28.2 323.4 %all-reduce.2.cloned.1.call-start = ((), (), s32[]{:S(2)}) async-start(), calls=%async_computation.2 | async-start | bytes 524288 | tf_op jit(solution)/shard_map/psum | solution.py:30
  29.6 438.8 %all-gather.2.cloned.1.call-start = ((), (), s32[]{:S(2)}) async-start(), calls=%async_computation.4 | async-start | bytes 6635520 | tf_op jit(solution)/shard_map/all_gather | solution.py:23
  30.8 563.2 %reduce-scatter.2.cloned.1.call-start = ((), (), s32[]{:S(2)}) async-start(), calls=%async_computation.3 | async-start | bytes 13271040 | tf_op jit(solution)/shard_map/reduce_scatter | solution.py:43
  364.0 7.9 %copy-start.5 = (bf16[1,128,4608]{2,0,1:T(2,128)(2,1)S(1)}, bf16[1,128,4608]{2,0,1:T(2,128)(2,1)}, u32[]{:S(2)}) copy-start(bf16[1,128,4608]{2,0,1:T(2,128)(2,1)} %get-tuple-element.14) | copy-start | bytes 3538948
  372.0 6.1 %copy-start.4 = (bf16[1,128,4608]{2,0,1:T(2,128)(2,1)S(1)}, bf16[1,128,4608]{2,0,1:T(2,128)(2,1)}, u32[]{:S(2)}) copy-start(bf16[1,128,4608]{2,0,1:T(2,128)(2,1)} %get-tuple-element.15) | copy-start | bytes 3538948
  378.1 6.1 %copy-start.3 = (bf16[1,128,4608]{2,0,1:T(2,128)(2,1)S(1)}, bf16[1,128,4608]{2,0,1:T(2,128)(2,1)}, u32[]{:S(2)}) copy-start(bf16[1,128,4608]{2,0,1:T(2,128)(2,1)} %get-tuple-element.16) | copy-start | bytes 3538948
  384.1 6.2 %copy-start.2 = (bf16[1,128,4608]{2,0,1:T(2,128)(2,1)S(1)}, bf16[1,128,4608]{2,0,1:T(2,128)(2,1)}, u32[]{:S(2)}) copy-start(bf16[1,128,4608]{2,0,1:T(2,128)(2,1)} %get-tuple-element.17) | copy-start | bytes 3538948
  390.4 6.1 %copy-start.1 = (bf16[1,128,4608]{2,0,1:T(2,128)(2,1)S(1)}, bf16[1,128,4608]{2,0,1:T(2,128)(2,1)}, u32[]{:S(2)}) copy-start(bf16[1,128,4608]{2,0,1:T(2,128)(2,1)} %get-tuple-element.18) | copy-start | bytes 3538948
  402.5 6.0 copy-start.6
Sparse Core Ops, SparseCore 0:
  32.2 319.3 all-reduce.1
Sparse Core Ops, SparseCore 1:
  33.2 129.5 all-gather.1
  445.0 148.9 reduce-scatter.1
